TPU v7x, 256 devices: a whole 4x4x8 slice. The times are simulated.
256 devices in a mesh: seq: 32 (over x, z), tp: 8 (over y, core).
Axes of the slice: x: 4, y: 4, z: 8, core: 2. Of those that a mesh axis runs over, the one named last changes fastest.
Arguments:
- event_vectors: bfloat16 [16384, 6144], P('seq'), may hold values from -6 to 6
- question_projector: bfloat16 [6144, 4096], P('seq', 'tp'), may hold values from -0.078125 to 0.078125
- lookup_projector: bfloat16 [6144, 4096], P('seq', 'tp'), may hold values from -0.078125 to 0.078125
- content_projector: bfloat16 [6144, 4096], P('seq', 'tp'), may hold values from -0.078125 to 0.078125
- channel_fading_speed: float32 [32], P('tp'), may hold values from 1.2207031e-05 to 0.03334
- surge_fading: float32 [16384], P('seq'), may hold values from -0.6932 to 0, as said below
- channel_scaling_coefficient: float32 [4096], P('tp'), may hold values from 0.1 to 1.9
- final_projector: bfloat16 [4096, 6144], P('seq', 'tp'), may hold values from -0.09375 to 0.09375
Outputs:
- mixed: bfloat16 [16384, 6144], P('seq', 'tp')
Inputs may be any that keep to these rules, and one draw needn't show every extreme that they name: `surge_fading`: zero at all but a few positions of the sequence.
All inputs are finite; a program needn't handle non-finite values.
Results may differ from a plain program's by a relative error of at most 0.0063.
Values may be sent and summed in bfloat16 or wider, within the bound.
A program may use at most 128 MiB of HBM per device.

v0:
```python
import jax
import jax.numpy as jnp
from jax import lax
from jax.sharding import PartitionSpec as P

HD = 128
SPAN_LENGTH = 512


def entering(part, axis, combine, identity):
    place = lax.axis_index(axis)
    gathered = jax.tree.map(lambda a: lax.all_gather(a, axis), part)
    state = jax.tree.map(lambda a, e: jnp.zeros_like(a) + jnp.asarray(e, a.dtype), part, identity)

    def one(step, state):
        return combine(
            state, jax.tree.map(lambda a: lax.dynamic_index_in_dim(a, step, 0, False), gathered)
        )

    return lax.fori_loop(0, place, one, state)


def block_pass(carry, inputs):
    carried, before = carry
    query_block, key_block, value_block, log_block = inputs
    inside = jnp.cumsum(log_block, axis=0)
    block_total = inside[-1]
    highest = lax.Precision.HIGHEST
    scores = jnp.einsum("thd,shd->hts", query_block, key_block, precision=highest)
    spread_log = inside.T[:, :, None] - inside.T[:, None, :]
    rows_index = lax.broadcasted_iota(jnp.int32, (SPAN_LENGTH, SPAN_LENGTH), 0)
    cols_index = lax.broadcasted_iota(jnp.int32, (SPAN_LENGTH, SPAN_LENGTH), 1)
    causal = (rows_index >= cols_index)[None, :, :]
    weight = jnp.where(causal, jnp.exp(jnp.where(causal, spread_log, 0.0)), 0.0)
    within = jnp.einsum("hts,shd->thd", scores * weight, value_block, precision=highest)
    across = jnp.einsum(
        "thd,hde->the", query_block * jnp.exp(inside)[:, :, None], carried, precision=highest
    )
    updated = jnp.exp(block_total)[:, None, None] * carried + jnp.einsum(
        "shd,she->hde",
        key_block * jnp.exp(block_total[None, :] - inside)[:, :, None],
        value_block,
        precision=highest,
    )
    factor = jnp.exp(before[None, :] + inside)
    return ((updated, before + block_total), (within + across, factor))


def chain_combine(earlier, later):
    return (earlier[0] + later[0], jnp.exp(later[0])[:, None, None] * earlier[1] + later[1])


def local(
    event_vectors,
    question_projector,
    lookup_projector,
    content_projector,
    channel_fading_speed,
    surge_fading,
    channel_scaling_coefficient,
    final_projector,
):
    tok_count = event_vectors.shape[0]
    number_of_heads = channel_fading_speed.shape[0]

    def project_rows(shard_rows):
        return jnp.dot(event_vectors, shard_rows, preferred_element_type=jnp.float32)

    query_sum = project_rows(lax.all_gather(question_projector, "seq", axis=0, tiled=True))
    key_sum = project_rows(lax.all_gather(lookup_projector, "seq", axis=0, tiled=True))
    value_sum = project_rows(lax.all_gather(content_projector, "seq", axis=0, tiled=True))
    queries = jax.nn.silu(query_sum).astype(jnp.bfloat16)
    keys_act = jax.nn.silu(key_sum).astype(jnp.bfloat16)
    values_act = value_sum.astype(jnp.bfloat16)
    span_count = tok_count // SPAN_LENGTH
    shaped = (span_count, SPAN_LENGTH, number_of_heads, HD)
    query_blocks = queries.astype(jnp.float32).reshape(shaped)
    key_blocks = keys_act.astype(jnp.float32).reshape(shaped)
    value_blocks = values_act.astype(jnp.float32).reshape(shaped)
    stepwise_fading_exponent = (surge_fading[:, None] - channel_fading_speed[None, :]).reshape(
        (span_count, SPAN_LENGTH, number_of_heads)
    )
    start = (
        jnp.zeros((number_of_heads, HD, HD), jnp.float32),
        jnp.zeros((number_of_heads,), jnp.float32),
    )
    (local_state, local_log), (outputs, factors) = lax.scan(
        block_pass, start, (query_blocks, key_blocks, value_blocks, stepwise_fading_exponent)
    )
    identity = (
        jnp.zeros((number_of_heads,), jnp.float32),
        jnp.zeros((number_of_heads, HD, HD), jnp.float32),
    )
    prior_log, incoming = entering((local_log, local_state), "seq", chain_combine, identity)
    query_flat = query_blocks.reshape((tok_count, number_of_heads, HD))
    reached = jnp.einsum("thd,hde->the", query_flat, incoming, precision=lax.Precision.HIGHEST)
    attention = (
        outputs.reshape((tok_count, number_of_heads, HD))
        + factors.reshape((tok_count, number_of_heads))[:, :, None] * reached
    )
    meansq = jnp.mean(attention * attention, axis=-1, keepdims=True)
    normed = (
        attention
        / jnp.sqrt(meansq + 1e-05)
        * channel_scaling_coefficient.reshape((number_of_heads, HD))[None, :, :]
    )
    normed = normed.reshape((tok_count, number_of_heads * HD)).astype(jnp.bfloat16)
    every_head = lax.all_gather(normed, "tp", axis=1, tiled=True)
    mixed = jnp.dot(
        every_head,
        lax.all_gather(final_projector, "seq", axis=0, tiled=True),
        preferred_element_type=jnp.float32,
    )
    return mixed.astype(jnp.bfloat16)


def solution(mesh):
    in_specs = (
        P("seq", None),
        P("seq", "tp"),
        P("seq", "tp"),
        P("seq", "tp"),
        P("tp"),
        P("seq"),
        P("tp"),
        P("seq", "tp"),
    )
    out_specs = P("seq", "tp")
    return jax.shard_map(local, mesh=mesh, in_specs=in_specs, out_specs=out_specs, check_vma=False)
```

profile of v0, /device:TPU:1, one launch (start us, length us, event | category | flops | bytes accessed | tf_op | source)
XLA Modules:
  0.0 514.1 jit_solution(17631043664003188020)
XLA Ops:
  6.5 0.0 all-gather.9.cloned.1.call-start
  6.5 0.7 all-gather.9.cloned.1.call-update
  7.3 0.0 all-gather.13.cloned.1.call-start
  7.3 0.7 all-gather.13.cloned.1.call-update
  8.0 0.0 all-gather.11.cloned.1.call-start
  8.1 0.7 all-gather.11.cloned.1.call-update
  8.7 0.0 all-gather.19.cloned.1.call-start
  8.8 0.8 broadcast_subtract_fusion
  9.6 1.2 reduce-window.6
  10.8 0.2 slice_reduce_fusion
  10.9 0.2 reduce-window.9
  11.1 0.1 add_bitcast_fusion
  11.2 0.2 slice_reduce_fusion.1
  11.4 0.1 subtract_exponential_fusion
  11.5 90.6 %all-gather.9.cloned.1.call-done = bf16[6144,512]{1,0:T(8,128)(2,1)} async-done(((bf16[192,512]{1,0:T(8,128)(2,1)}), bf16[6144,512]{1,0:T(8,128)(2,1)}) %all-gather.9.cloned.1.call-update) | async-done | bytes 6291472 | tf_op jit(solution)/shard_map/all_gather | solution.py:71
  102.1 8.1 %convolution_convert_fusion.1 = bf16[512,512]{0,1:T(8,128)(2,1)S(1)} fusion(bf16[512,6144]{1,0:T(8,128)(2,1)} %param.10, bf16[6144,512]{1,0:T(8,128)(2,1)} %all-gather.9.cloned.1.call-done), kind=kOutput, calls=%fused_computation.18 | convolution fusion | flops 3221487616 | bytes 13107200 | tf_op jit(solution)/shard_map/dot_general | solution.py:67
  110.2 80.2 %all-gather.13.cloned.1.call-done = bf16[6144,512]{1,0:T(8,128)(2,1)} async-done(((bf16[192,512]{1,0:T(8,128)(2,1)}), bf16[6144,512]{1,0:T(8,128)(2,1)}) %all-gather.13.cloned.1.call-update) | async-done | bytes 6291472 | tf_op jit(solution)/shard_map/all_gather | solution.py:70
  190.4 8.2 %multiply_convert_fusion.1 = bf16[512,512]{0,1:T(8,128)(2,1)S(1)} fusion(bf16[512,6144]{1,0:T(8,128)(2,1)} %param.10, bf16[6144,512]{1,0:T(8,128)(2,1)} %all-gather.13.cloned.1.call-done), kind=kOutput, calls=%fused_computation.27 | convolution fusion | flops 3222536192 | bytes 13107200 | tf_op jit(solution)/shard_map/dot_general | solution.py:67
  198.6 1.4 convolution_add_fusion.1
  199.9 0.0 all-gather.19.cloned.1.call-update
  200.0 0.0 all-gather.17.cloned.1.call-start
  200.0 0.5 all-gather.17.cloned.1.call-update
  200.6 0.0 all-gather.15.cloned.1.call-start
  200.6 31.6 %all-gather.1 = f32[32,1,4]{2,1,0:T(1,128)S(1)} all-gather(f32[1,1,4]{2,1,0:T(1,128)S(1)} %bitcast.69), channel_id=1, replica_groups=mesh['seq'=32,'tp'=8] {'seq'}, dimensions={0}, use_global_device_ids=true | all-gather | bytes 528 | tf_op jit(solution)/shard_map/all_gather | solution.py:12
  232.2 0.1 iota_compare_fusion
  232.3 46.4 %all-gather.11.cloned.1.call-done = bf16[6144,512]{1,0:T(8,128)(2,1)} async-done(((bf16[192,512]{1,0:T(8,128)(2,1)}), bf16[6144,512]{1,0:T(8,128)(2,1)}) %all-gather.11.cloned.1.call-update) | async-done | bytes 6291472 | tf_op jit(solution)/shard_map/all_gather | solution.py:69
  278.7 8.2 %multiply_convert_fusion.2 = bf16[512,512]{0,1:T(8,128)(2,1)S(1)} fusion(bf16[512,6144]{1,0:T(8,128)(2,1)} %param.10, bf16[6144,512]{1,0:T(8,128)(2,1)} %all-gather.11.cloned.1.call-done), kind=kOutput, calls=%fused_computation.28 | convolution fusion | flops 3222536192 | bytes 13107200 | tf_op jit(solution)/shard_map/dot_general | solution.py:67
  286.9 0.7 fusion.23
  287.6 3.7 fusion
  291.3 0.0 copy-start
  291.3 1.0 fusion.12
  292.4 84.0 %all-gather.19.cloned.1.call-done = f32[128,128,128]{2,1,0:T(8,128)} async-done(((f32[4,128,128]{2,1,0:T(8,128)}), f32[128,128,128]{2,1,0:T(8,128)}) %all-gather.19.cloned.1.call-update) | async-done | bytes 8388624 | tf_op jit(solution)/shard_map/all_gather | solution.py:12
  376.4 0.2 while.3
  376.6 0.7 multiply_reduce_fusion
  377.4 0.0 copy-done
  377.4 0.9 multiply_convert_fusion
  378.3 0.0 all-gather.15.cloned.1.call-update
  378.4 86.3 %all-gather.17.cloned.1.call-done = bf16[4096,768]{1,0:T(8,128)(2,1)} async-done(((bf16[128,768]{1,0:T(8,128)(2,1)}), bf16[4096,768]{1,0:T(8,128)(2,1)}) %all-gather.17.cloned.1.call-update) | async-done | bytes 6291472 | tf_op jit(solution)/shard_map/all_gather | solution.py:111
  464.6 34.2 %all-gather.15.cloned.1.call-done = bf16[512,4096]{0,1:T(8,128)(2,1)} async-done(((bf16[512,512]{0,1:T(8,128)(2,1)}), bf16[512,4096]{0,1:T(8,128)(2,1)}) %all-gather.15.cloned.1.call-update) | async-done | bytes 4194320 | tf_op jit(solution)/shard_map/all_gather | solution.py:108
  498.8 8.4 %convolution_convert_fusion = bf16[512,768]{1,0:T(8,128)(2,1)} fusion(bf16[512,4096]{0,1:T(8,128)(2,1)} %all-gather.15.cloned.1.call-done, bf16[4096,768]{1,0:T(8,128)(2,1)} %all-gather.17.cloned.1.call-done), kind=kOutput, calls=%fused_computation.12 | convolution fusion | flops 3221618688 | bytes 11272192 | tf_op jit(solution)/shard_map/dot_general | solution.py:109
  (4 shorter events, 0.0 us)
Async XLA Ops:
  6.5 95.6 %all-gather.9.cloned.1.call-start = ((), (), s32[]{:S(2)}) async-start(), calls=%async_computation | async-start | bytes 6488064 | tf_op jit(solution)/shard_map/all_gather | solution.py:71
  7.3 183.1 %all-gather.13.cloned.1.call-start = ((), (), s32[]{:S(2)}) async-start(), calls=%async_computation.2 | async-start | bytes 6488064 | tf_op jit(solution)/shard_map/all_gather | solution.py:70
  8.0 270.7 %all-gather.11.cloned.1.call-start = ((), (), s32[]{:S(2)}) async-start(), calls=%async_computation.1 | async-start | bytes 6488064 | tf_op jit(solution)/shard_map/all_gather | solution.py:69
  8.7 367.6 %all-gather.19.cloned.1.call-start = ((), (), s32[]{:S(2)}) async-start(), calls=%async_computation.5 | async-start | bytes 8650752 | tf_op jit(solution)/shard_map/all_gather | solution.py:12
  200.0 264.7 %all-gather.17.cloned.1.call-start = ((), (), s32[]{:S(2)}) async-start(), calls=%async_computation.4 | async-start | bytes 6488064 | tf_op jit(solution)/shard_map/all_gather | solution.py:111
  200.6 298.3 %all-gather.15.cloned.1.call-start = ((), (), s32[]{:S(2)}) async-start(), calls=%async_computation.3 | async-start | bytes 4718592 | tf_op jit(solution)/shard_map/all_gather | solution.py:108
  291.3 86.1 %copy-start = (f32[512]{0:T(512)S(1)}, f32[512]{0:T(512)}, u32[]{:S(2)}) copy-start(f32[512]{0:T(512)} %param.16) | copy-start | bytes 6148
Sparse Core Ops, SparseCore 0:
  9.9 92.1 all-gather.8
  104.7 85.6 all-gather.12
  192.9 85.6 all-gather.10
  281.1 95.1 all-gather.18
  378.8 85.8 all-gather.16
  466.3 32.4 all-gather.14
where the time goes:
time: 515 us; the launch traced here: 514 us
  waiting for transfers between devices  424 us (82%)
  matrix products  40.4 us (8%)
  blocking collectives  31.6 us (6%)
  between operations  13.6 us (3%)
    all_gather x1, waiting for transfers between devices, local(): lax.all_gather(content_projector, 'seq', axis=0, tiled=True)  90.6 us
    all_gather x1, waiting for transfers between devices, local(): lax.all_gather(final_projector, 'seq', axis=0, tiled=True)  86.3 us
    all_gather x1, waiting for transfers between devices, entering(): gathered = jax.tree.map(lambda a: lax.all_gather(a, axis), part)  84 us
    all_gather x1, waiting for transfers between devices, local(): lax.all_gather(lookup_projector, 'seq', axis=0, tiled=True)  80.2 us
    all_gather x1, waiting for transfers between devices, local(): lax.all_gather(question_projector, 'seq', axis=0, tiled=True)  46.4 us
    all_gather x1, waiting for transfers between devices, local(): every_head = lax.all_gather(normed, 'tp', axis=1, tiled=True)  34.2 us
    all_gather x1, blocking collectives, entering(): gathered = jax.tree.map(lambda a: lax.all_gather(a, axis), part)  31.6 us
    dot_general x3, matrix products, project_rows(): jnp.dot(event_vectors, shard_rows, preferred_element_type=jnp.float32)  24.4 us
  transfers between devices with their start and end apart: 6, of which 6 were waited for; matrix products, arithmetic and copies ran while one was open for 7% of the time, Pallas kernels for 0%

commit v1 on v0

--- a/solution.py
+++ b/solution.py
@@ -108,7 +108,9 @@
     every_head = lax.all_gather(normed, "tp", axis=1, tiled=True)
     mixed = jnp.dot(
         every_head,
-        lax.all_gather(final_projector, "seq", axis=0, tiled=True),
+        jnp.concatenate(
+            lax.all_to_all(jnp.stack([final_projector] * lax.axis_size("seq")), "seq", 0, 0), axis=0
+        ),
         preferred_element_type=jnp.float32,
     )
     return mixed.astype(jnp.bfloat16)

time: 515 us -> 544 us (1.056)
  blocking collectives: 31.6 us -> 203 us
  waiting for transfers between devices: 424 us -> 273 us
    all_gather x1, blocking collectives: 31.6 us -> 203 us  [entering(): gathered = jax.tree.map(lambda a: lax.all_gather(a, axis), part)]
    all_gather x1 -> x0, waiting for transfers between devices: 86.3 us -> none  [local(): lax.all_gather(final_projector, 'seq', axis=0, tiled=True)]
    all_gather x1, waiting for transfers between devices: 84 us -> 35.2 us  [entering(): gathered = jax.tree.map(lambda a: lax.all_gather(a, axis), part)]
    all_gather x1, waiting for transfers between devices: 46.4 us -> 0.02 us  [local(): lax.all_gather(question_projector, 'seq', axis=0, tiled=True)]
    all_gather x1, waiting for transfers between devices: 34.2 us -> 64.6 us  [local(): every_head = lax.all_gather(normed, 'tp', axis=1, tiled=True)]
  transfers between devices with their start and end apart: 6 -> 6, of which waited for: 6 -> 4; matrix products, arithmetic and copies ran while one was open for 7% -> 7% of each run, Pallas kernels for 0% -> 0%
where the time goes in v1:
time: 544 us; the launch traced here: 543 us
  waiting for transfers between devices  273 us (50%)
  blocking collectives  203 us (37%)
  matrix products  41 us (8%)
  between operations  13.3 us (2%)
  starting transfers between devices  5.57 us (1%)
    all_gather x1, blocking collectives, entering(): gathered = jax.tree.map(lambda a: lax.all_gather(a, axis), part)  203 us
    all_gather x1, waiting for transfers between devices, local(): lax.all_gather(content_projector, 'seq', axis=0, tiled=True)  90.6 us
    all_gather x1, waiting for transfers between devices, local(): lax.all_gather(lookup_projector, 'seq', axis=0, tiled=True)  80.2 us
    all_gather x1, waiting for transfers between devices, local(): every_head = lax.all_gather(normed, 'tp', axis=1, tiled=True)  64.6 us
    all_gather x1, waiting for transfers between devices, entering(): gathered = jax.tree.map(lambda a: lax.all_gather(a, axis), part)  35.2 us
    dot_general x3, matrix products, project_rows(): jnp.dot(event_vectors, shard_rows, preferred_element_type=jnp.float32)  25 us
  transfers between devices with their start and end apart: 6, of which 4 were waited for; matrix products, arithmetic and copies ran while one was open for 7% of the time, Pallas kernels for 0%

profile of v1, /device:TPU:1, one launch (start us, length us, event | category | flops | bytes accessed | tf_op | source)
XLA Modules:
  0.0 542.8 jit_solution(9116140395271626068)
XLA Ops:
  6.5 0.0 all-gather.8.cloned.1.call-start
  6.5 0.7 all-gather.8.cloned.1.call-update
  7.3 0.0 all-gather.12.cloned.1.call-start
  7.3 0.7 all-gather.12.cloned.1.call-update
  8.0 0.0 all-gather.10.cloned.1.call-start
  8.1 0.7 all-gather.10.cloned.1.call-update
  8.7 0.0 all-gather.16.cloned.1.call-start
  8.8 0.8 broadcast_subtract_fusion
  9.6 1.2 reduce-window.6
  10.8 0.2 slice_reduce_fusion
  10.9 0.2 reduce-window.9
  11.1 0.1 add_bitcast_fusion
  11.2 0.2 slice_reduce_fusion.1
  11.4 0.1 subtract_exponential_fusion
  11.5 90.6 %all-gather.8.cloned.1.call-done = bf16[6144,512]{1,0:T(8,128)(2,1)} async-done(((bf16[192,512]{1,0:T(8,128)(2,1)}), bf16[6144,512]{1,0:T(8,128)(2,1)}) %all-gather.8.cloned.1.call-update) | async-done | bytes 6291472 | tf_op jit(solution)/shard_map/all_gather | solution.py:71
  102.1 8.1 %convolution_convert_fusion.1 = bf16[512,512]{0,1:T(8,128)(2,1)S(1)} fusion(bf16[512,6144]{1,0:T(8,128)(2,1)} %param.10, bf16[6144,512]{1,0:T(8,128)(2,1)} %all-gather.8.cloned.1.call-done), kind=kOutput, calls=%fused_computation.18 | convolution fusion | flops 3221487616 | bytes 13107200 | tf_op jit(solution)/shard_map/dot_general | solution.py:67
  110.2 0.0 copy-start
  110.2 80.2 %all-gather.12.cloned.1.call-done = bf16[6144,512]{1,0:T(8,128)(2,1)} async-done(((bf16[192,512]{1,0:T(8,128)(2,1)}), bf16[6144,512]{1,0:T(8,128)(2,1)}) %all-gather.12.cloned.1.call-update) | async-done | bytes 6291472 | tf_op jit(solution)/shard_map/all_gather | solution.py:70
  190.4 8.2 %multiply_convert_fusion.1 = bf16[512,512]{0,1:T(8,128)(2,1)S(1)} fusion(bf16[512,6144]{1,0:T(8,128)(2,1)} %param.10, bf16[6144,512]{1,0:T(8,128)(2,1)} %all-gather.12.cloned.1.call-done), kind=kOutput, calls=%fused_computation.27 | convolution fusion | flops 3222536192 | bytes 13107200 | tf_op jit(solution)/shard_map/dot_general | solution.py:67
  198.6 1.4 convolution_add_fusion.1
  199.9 0.0 all-gather.16.cloned.1.call-update
  200.0 0.0 copy-done
  200.0 3.3 stack.2
  203.3 5.4 all-to-all-start
  208.7 0.0 all-gather.14.cloned.1.call-start
  208.7 202.9 %all-gather.1 = f32[32,1,4]{2,1,0:T(1,128)S(1)} all-gather(f32[1,1,4]{2,1,0:T(1,128)S(1)} %bitcast.70), channel_id=1, replica_groups=mesh['seq'=32,'tp'=8] {'seq'}, dimensions={0}, use_global_device_ids=true | all-gather | bytes 528 | tf_op jit(solution)/shard_map/all_gather | solution.py:12
  411.7 0.1 iota_compare_fusion
  411.7 0.0 all-gather.10.cloned.1.call-done
  411.8 8.7 %multiply_convert_fusion.2 = bf16[512,512]{0,1:T(8,128)(2,1)S(1)} fusion(bf16[512,6144]{1,0:T(8,128)(2,1)} %param.10, bf16[6144,512]{1,0:T(8,128)(2,1)} %all-gather.10.cloned.1.call-done), kind=kOutput, calls=%fused_computation.28 | convolution fusion | flops 3222536192 | bytes 13107200 | tf_op jit(solution)/shard_map/dot_general | solution.py:67
  420.5 0.7 fusion.23
  421.3 3.7 fusion
  425.0 0.0 copy-start.1
  425.0 1.0 fusion.12
  426.0 35.2 %all-gather.16.cloned.1.call-done = f32[128,128,128]{2,1,0:T(8,128)} async-done(((f32[4,128,128]{2,1,0:T(8,128)}), f32[128,128,128]{2,1,0:T(8,128)}) %all-gather.16.cloned.1.call-update) | async-done | bytes 8388624 | tf_op jit(solution)/shard_map/all_gather | solution.py:12
  461.2 0.2 while.3
  461.5 0.7 multiply_reduce_fusion
  462.2 0.0 copy-done.1
  462.2 0.9 multiply_convert_fusion
  463.2 0.0 all-gather.14.cloned.1.call-update
  463.2 0.0 all-to-all-done
  463.2 64.6 %all-gather.14.cloned.1.call-done = bf16[512,4096]{0,1:T(8,128)(2,1)} async-done(((bf16[512,512]{0,1:T(8,128)(2,1)}), bf16[512,4096]{0,1:T(8,128)(2,1)}) %all-gather.14.cloned.1.call-update) | async-done | bytes 4194320 | tf_op jit(solution)/shard_map/all_gather | solution.py:108
  527.9 8.4 %convolution_convert_fusion = bf16[512,768]{1,0:T(8,128)(2,1)} fusion(bf16[512,4096]{0,1:T(8,128)(2,1)} %all-gather.14.cloned.1.call-done, bf16[4096,768]{1,0:T(8,128)(2,1)} %bitcast.13), kind=kOutput, calls=%fused_computation.12 | convolution fusion | flops 3221618688 | bytes 11272192 | tf_op jit(solution)/shard_map/dot_general | solution.py:109
  (4 shorter events, 0.0 us)
Async XLA Ops:
  6.5 95.6 %all-gather.8.cloned.1.call-start = ((), (), s32[]{:S(2)}) async-start(), calls=%async_computation.1 | async-start | bytes 6488064 | tf_op jit(solution)/shard_map/all_gather | solution.py:71
  7.3 183.1 %all-gather.12.cloned.1.call-start = ((), (), s32[]{:S(2)}) async-start(), calls=%async_computation.3 | async-start | bytes 6488064 | tf_op jit(solution)/shard_map/all_gather | solution.py:70
  8.0 403.8 %all-gather.10.cloned.1.call-start = ((), (), s32[]{:S(2)}) async-start(), calls=%async_computation.2 | async-start | bytes 6488064 | tf_op jit(solution)/shard_map/all_gather | solution.py:69
  8.7 452.5 %all-gather.16.cloned.1.call-start = ((), (), s32[]{:S(2)}) async-start(), calls=%async_computation.5 | async-start | bytes 8650752 | tf_op jit(solution)/shard_map/all_gather | solution.py:12
  110.2 89.8 %copy-start = (bf16[128,768]{1,0:T(8,128)(2,1)S(1)}, bf16[128,768]{1,0:T(8,128)(2,1)}, u32[]{:S(2)}) copy-start(bf16[128,768]{1,0:T(8,128)(2,1)} %param.17) | copy-start | bytes 589828
  203.3 260.0 %all-to-all-start = ((bf16[32,128,768]{2,1,0:T(8,128)(2,1)}), bf16[32,128,768]{2,1,0:T(8,128)(2,1)}, u32[]{:S(2)}, u32[]{:S(2)}) async-start(bf16[32,128,768]{2,1,0:T(8,128)(2,1)} %stack.2), calls=%async_computation | async-start | bytes 12582912 | tf_op jit(solution)/shard_map/all_to_all | solution.py:112
  208.7 319.2 %all-gather.14.cloned.1.call-start = ((), (), s32[]{:S(2)}) async-start(), calls=%async_computation.4 | async-start | bytes 4718592 | tf_op jit(solution)/shard_map/all_gather | solution.py:108
  425.0 37.3 %copy-start.1 = (f32[512]{0:T(512)S(1)}, f32[512]{0:T(512)}, u32[]{:S(2)}) copy-start(f32[512]{0:T(512)} %param.16) | copy-start | bytes 6148
Sparse Core Ops, SparseCore 0:
  9.9 92.1 all-gather.7
  104.7 85.6 all-gather.11
  192.9 161.2 all-gather.9
  356.7 104.4 all-gather.15
  463.3 64.4 all-gather.13
